TPU v7x, 32 devices: a whole 2x2x4 slice. The times are simulated.
32 devices in a mesh: grp: 2 (over x), ctx: 16 (over z, y, core).
Axes of the slice: x: 2, y: 2, z: 4, core: 2. Of those that a mesh axis runs over, the one named last changes fastest.
Arguments:
- queries: bfloat16 [960, 4096], P(None, ('grp', 'ctx')), parts along dimension 1, may hold values from -6 to 6
- key_rows: bfloat16 [960, 4096], P(None, ('grp', 'ctx')), parts along dimension 1, may hold values from -6 to 6
- value_rows: bfloat16 [960, 4096], P(None, ('grp', 'ctx')), parts along dimension 1, may hold values from -6 to 6
- short_taps: float32 [3, 960, 7], replicated, may hold values from -2 to 2
- long_filter: bfloat16 [960, 2048], P('ctx'), may hold values from -0.125 to 0.125
Outputs:
- mixed: bfloat16 [960, 4096], P(None, ('grp', 'ctx')), parts along dimension 1
There are 2 independent parts, one for each index of `grp`. A program takes and returns all parts, laid end to end along the dimension named above; an argument that names none is the same for every part. Nothing has to cross between parts.
All inputs are finite; a program needn't handle non-finite values.
Results may differ from a plain program's by a relative error of at most 0.0057.
Values may be sent and summed in bfloat16 or wider, within the bound.
A program may use at most 64 MiB of HBM per device.

v0:
```python
import math
import jax
import jax.numpy as jnp
from jax import lax
from jax.sharding import PartitionSpec as P

TAPS = 7
precise = lax.Precision.HIGH


def with_halo(value, sides, width):
    for axis, dim in sides:
        size, length = (lax.axis_size(axis), value.shape[dim])
        up = [(i, (i + 1) % size) for i in range(size - 1)]
        down = [(j, i) for i, j in up]
        last = lax.slice_in_dim(value, length - width, length, axis=dim)
        leading = lax.slice_in_dim(value, 0, width, axis=dim)
        before = lax.ppermute(last, axis, up)
        after = lax.ppermute(leading, axis, down)
        value = jnp.concatenate([before, value, after], axis=dim)
    return value


def angles(count_rows, count_cols, modulus):
    row_ids = lax.broadcasted_iota(jnp.int32, (count_rows, count_cols), 0)
    col_ids = lax.broadcasted_iota(jnp.int32, (count_rows, count_cols), 1)
    phase = (row_ids * col_ids % modulus).astype(jnp.float32) * (2.0 * math.pi / modulus)
    return (jnp.cos(phase), jnp.sin(phase))


def fourier_tables(length):
    inner_len = min(128, length)
    padded_len = 2 * length
    outer_len = padded_len // inner_len
    cos_outer, sin_outer = angles(outer_len // 2, outer_len, outer_len)
    cos_twist, sin_twist = angles(outer_len, inner_len, padded_len)
    cos_inner, sin_inner = angles(inner_len, inner_len, inner_len)
    outer_fwd = jnp.stack([cos_outer, -sin_outer])
    inner_fwd = jnp.stack([jnp.stack([cos_inner, -sin_inner]), jnp.stack([sin_inner, cos_inner])])
    inner_inv = jnp.stack([jnp.stack([cos_inner, sin_inner]), jnp.stack([-sin_inner, cos_inner])])
    return (outer_fwd, cos_twist, sin_twist, inner_fwd, inner_inv, padded_len)


def forward(signal, tables):
    outer_fwd, cos_twist, sin_twist, inner_fwd, inner_inv, padded_len = tables
    shaped = signal.reshape(signal.shape[:-1] + (outer_fwd.shape[1], inner_fwd.shape[2]))
    first = jnp.einsum("...ab,caf->...cfb", shaped, outer_fwd, precision=precise)
    first_real = first[..., 0, :, :]
    first_imag = first[..., 1, :, :]
    twist = jnp.stack(
        [
            first_real * cos_twist + first_imag * sin_twist,
            first_imag * cos_twist - first_real * sin_twist,
        ],
        axis=-3,
    )
    return jnp.einsum("...cfb,cdbk->...dfk", twist, inner_fwd, precision=precise)


def inverse(spectrum, tables):
    outer_fwd, cos_twist, sin_twist, inner_fwd, inner_inv, padded_len = tables
    first = jnp.einsum("...cfk,cdkb->...dfb", spectrum, inner_inv, precision=precise)
    first_real = first[..., 0, :, :]
    first_imag = first[..., 1, :, :]
    twist = jnp.stack(
        [
            first_real * cos_twist - first_imag * sin_twist,
            first_imag * cos_twist + first_real * sin_twist,
        ],
        axis=-3,
    )
    result = jnp.einsum("...cfb,caf->...ab", twist, outer_fwd, precision=precise)
    result = result / padded_len
    return result.reshape(result.shape[:-2] + (result.shape[-2] * result.shape[-1],))


def on_device(queries, key_rows, value_rows, short_taps, long_filter):
    tokens = queries.shape[1]
    rim_width = TAPS - 1
    stacked = jnp.stack([queries, key_rows, value_rows])
    padded = with_halo(stacked, (("ctx", 2),), rim_width)
    mirrored_taps = short_taps[:, ::-1, :]
    causal = jnp.zeros(stacked.shape, jnp.float32)
    anticausal = jnp.zeros(stacked.shape, jnp.float32)
    for offset in range(TAPS):
        begin = rim_width - offset
        causal = causal + short_taps[:, :, offset, None] * padded[:, :, begin : begin + tokens]
        later = rim_width + offset
        anticausal = (
            anticausal + mirrored_taps[:, :, offset, None] * padded[:, :, later : later + tokens]
        )
    product_a = (causal[1] * causal[2]).astype(jnp.bfloat16)
    product_b = (anticausal[1] * anticausal[2]).astype(jnp.bfloat16)
    tables = fourier_tables(long_filter.shape[1])
    outgoing = jnp.stack([product_a, product_b[::-1]])
    channel_rows = lax.all_to_all(outgoing, "ctx", split_axis=1, concat_axis=2, tiled=True)
    filter_spec = forward(long_filter.astype(jnp.float32), tables)
    data_spec = forward(channel_rows.astype(jnp.float32), tables)
    filter_real = filter_spec[:, 0]
    filter_imag = filter_spec[:, 1]
    data_real = data_spec[:, :, 0]
    data_imag = data_spec[:, :, 1]
    first_real = filter_real * data_real[0] - filter_imag * data_imag[0]
    first_imag = filter_real * data_imag[0] + filter_imag * data_real[0]
    second_real = filter_real * data_real[1] + filter_imag * data_imag[1]
    second_imag = filter_real * data_imag[1] - filter_imag * data_real[1]
    spectrum = jnp.stack(
        [jnp.stack([first_real, first_imag], axis=1), jnp.stack([second_real, second_imag], axis=1)]
    )
    convolved = inverse(spectrum, tables).astype(jnp.bfloat16)
    token_rows = lax.all_to_all(convolved, "ctx", split_axis=2, concat_axis=1, tiled=True)
    mixed_b = token_rows[1][::-1]
    result = causal[0] * token_rows[0].astype(jnp.float32) + anticausal[0] * mixed_b.astype(
        jnp.float32
    )
    return result.astype(jnp.bfloat16)


def solution(mesh):
    placed = (
        P(None, ("grp", "ctx")),
        P(None, ("grp", "ctx")),
        P(None, ("grp", "ctx")),
        P(),
        P("ctx", None),
    )
    return jax.shard_map(
        on_device, mesh=mesh, in_specs=placed, out_specs=P(None, ("grp", "ctx")), check_vma=False
    )
```

profile of v0, /device:TPU:0, one launch (start us, length us, event | category | flops | bytes accessed | tf_op | source)
XLA Modules:
  0.0 102.4 jit_solution(13261690223920789769)
XLA Ops:
  0.0 1.3 %pad_maximum_fusion.2 = bf16[3,960,128]{2,1,0:T(8,128)(2,1)S(1)} fusion(bf16[1,960,128]{2,1,0:T(8,128)(2,1)} %bitcast.184, bf16[1,960,128]{2,1,0:T(8,128)(2,1)} %bitcast.188, bf16[1,960,128]{2,1,0:T(8,128)(2,1)} %bitcast.192), kind=kLoop, calls=%fused_computation.55 | loop fusion | flops 737280 | bytes 1474560 | tf_op jit(solution)/shard_map/stack | solution.py:80
  1.3 0.3 fusion.94
  1.6 0.3 copy.51
  1.9 1.3 %collective-permute-start.1 = (bf16[3,960,6]{1,2,0:T(8,128)(2,1)S(1)}, bf16[3,960,6]{1,2,0:T(8,128)(2,1)S(1)}, u32[]{:S(2)}, u32[]{:S(2)}) collective-permute-start(bf16[3,960,6]{1,2,0:T(8,128)(2,1)S(1)} %copy.51), channel_id=1, source_target_pairs={{1,0},{2,1},{3,2},{4,3},{5,4},{6,5},{7,6},{8,7},{9,8},{10,9},{11,1... | collective-permute-start | bytes 103688 | tf_op jit(solution)/shard_map/ppermute | solution.py:19
  3.2 0.3 copy.47
  3.5 3.0 %collective-permute-start = (bf16[3,960,6]{1,2,0:T(8,128)(2,1)S(1)}, bf16[3,960,6]{1,2,0:T(8,128)(2,1)S(1)}, u32[]{:S(2)}, u32[]{:S(2)}) collective-permute-start(bf16[3,960,6]{1,2,0:T(8,128)(2,1)S(1)} %copy.47), channel_id=1, source_target_pairs={{0,1},{1,2},{2,3},{3,4},{4,5},{5,6},{6,7},{7,8},{8,9},{9,10},{10,1... | collective-permute-start | bytes 103688 | tf_op jit(solution)/shard_map/ppermute | solution.py:18
  6.6 0.3 fusion.70
  6.9 0.3 fusion.68
  7.3 0.7 reverse.8
  8.0 0.1 slice.344
  8.1 0.7 reverse.7
  8.9 0.1 slice.343
  9.0 0.7 reverse.12
  9.7 0.1 slice.348
  9.8 0.6 copy_bitcast_fusion.11
  10.4 0.7 reverse.11
  11.1 0.1 slice.347
  11.2 0.7 reverse.10
  12.0 0.1 slice.346
  12.1 0.6 copy_bitcast_fusion.9
  12.7 0.7 reverse.9
  13.5 0.6 copy_bitcast_fusion
  14.1 0.6 copy_bitcast_fusion.4
  14.7 0.6 copy_bitcast_fusion.2
  15.4 0.7 fusion.60
  16.1 0.6 copy.140
  16.7 0.7 reverse.13
  17.5 0.1 slice.349
  17.6 0.6 copy.139
  18.2 0.4 copy.48
  18.7 1.2 %copy.52 = bf16[3,960,6]{2,1,0:T(8,128)(2,1)} copy(bf16[3,960,6]{1,2,0:T(8,128)(2,1)S(1)} %collective-permute-done.1) | data formatting | bytes 69120 | tf_op jit(solution)/shard_map/ppermute | solution.py:19
  19.9 2.5 %maximum_maximum_fusion = (bf16[3,960,134]{2,1,0:T(8,128)(2,1)S(1)}, bf16[3,960,134]{2,1,0:T(8,128)(2,1)S(1)}) fusion(bf16[1,960,128]{2,1,0:T(8,128)(2,1)S(1)} %bitcast.185, bf16[1,960,128]{2,1,0:T(8,128)(2,1)S(1)} %bitcast.189, bf16[1,960,128]{2,1,0:T(8,128)(2,1)S(1)} %bitcast.193, bf16[3,960,6]{2,1,0:T(8,128)(2,1)S(1)} %copy.48, bf16[3,960,6]{2,1,0:T(8,128)(2,1)} %copy.52), kind=kLoop, calls=%fused_computation.39 | loop fusion | flops 6174720 | bytes 2350080 | tf_op jit(solution)/shard_map/concatenate | solution.py:20
  22.6 4.5 %fusion.31 = f32[3,960,128]{2,1,0:T(8,128)S(1)} fusion(bf16[3,960,134]{2,1,0:T(8,128)(2,1)S(1)} %get-tuple-element.16, f32[3,960]{1,0:T(4,128)S(1)} %copy-done.13, f32[3,960]{1,0:T(4,128)S(1)} %copy-done.14, f32[3,960]{1,0:T(4,128)S(1)} %copy-done.17, f32[3,960]{1,0:T(4,128)S(1)} %copy-done.18, f32[3,960]{1,0:T(4,128)S(1)} %copy-done.15, ...), kind=kLoop, calls=%fused_computation.38 | loop fusion | flops 8110080 | bytes 6716160 | tf_op jit(solution)/shard_map/add | solution.py:90
  27.1 1.1 %copy-done = f32[3,960,128]{2,1,0:T(8,128)} copy-done((f32[3,960,128]{2,1,0:T(8,128)}, f32[3,960,128]{2,1,0:T(8,128)S(1)}, u32[]{:S(2)}) %copy-start) | copy-done | bytes 1474584
  28.3 0.6 rev.7
  29.0 4.3 %fusion.25 = f32[3,960,128]{2,1,0:T(8,128)S(1)} fusion(bf16[3,960,134]{2,1,0:T(8,128)(2,1)S(1)} %get-tuple-element.15, f32[3,960]{1,0:T(4,128)S(1)} %get-tuple-element.34, f32[3,960]{1,0:T(4,128)S(1)} %get-tuple-element.35, f32[3,960]{1,0:T(4,128)S(1)} %copy-done.11, f32[3,960]{1,0:T(4,128)S(1)} %copy-done.12, f32[3,960]{1,0:T(4,128)S(1)} %copy-done.9, ...), kind=kLoop, calls=%fused_computation.32 | loop fusion | flops 8110080 | bytes 6716160 | tf_op jit(solution)/shard_map/add | solution.py:87
  33.3 1.1 %copy-done.1 = f32[3,960,128]{2,1,0:T(8,128)} copy-done((f32[3,960,128]{2,1,0:T(8,128)}, f32[3,960,128]{2,1,0:T(8,128)S(1)}, u32[]{:S(2)}) %copy-start.1) | copy-done | bytes 1474584
  34.5 1.3 %copy.53 = bf16[2,960,128]{2,0,1:T(2,128)(2,1)} copy(bf16[2,960,128]{2,1,0:T(8,128)(2,1)S(1)} %pad_maximum_fusion.3) | data formatting | bytes 983040 | tf_op jit(solution)/shard_map/stack | solution.py:95
  35.8 8.1 %all-to-all-start = ((bf16[2,960,128]{2,0,1:T(2,128)(2,1)}), bf16[2,960,128]{2,0,1:T(2,128)(2,1)S(1)}, u32[]{:S(2)}, u32[]{:S(2)}) async-start(bf16[2,960,128]{2,0,1:T(2,128)(2,1)} %copy.53), calls=%async_computation | async-start | bytes 983040 | tf_op jit(solution)/shard_map/all_to_all | solution.py:96
  44.0 0.7 convolution_bitcast_fusion.1
  44.7 0.3 multiply_add_fusion.4
  45.0 0.2 pad_maximum_fusion
  45.2 2.0 %fusion.17 = f32[60,2,32,128]{3,0,2,1:T(8,128)S(1)} fusion(f32[60,2,32,128]{3,2,0,1:T(8,128)S(1)} %pad_maximum_fusion, f32[1,2,128,128]{3,2,0,1:T(8,128)S(1)} %get-tuple-element.22, f32[1,2,128,128]{3,2,0,1:T(8,128)S(1)} %get-tuple-element.32), kind=kOutput, calls=%fused_computation.25 | convolution fusion | flops 755040256 | bytes 4194304 | tf_op jit(solution)/shard_map/...cfb,cdbk->...dfk/dot_general | solution.py:57
  47.2 10.4 %all-to-all-done = bf16[2,960,128]{2,0,1:T(2,128)(2,1)S(1)} async-done(((bf16[2,960,128]{2,0,1:T(2,128)(2,1)}), bf16[2,960,128]{2,0,1:T(2,128)(2,1)S(1)}, u32[]{:S(2)}, u32[]{:S(2)}) %all-to-all-start) | async-done | bytes 491552 | tf_op jit(solution)/shard_map/all_to_all | solution.py:96
  57.6 1.2 %convolution_bitcast_fusion = f32[2,60,2,32,128]{4,3,1,0,2:T(8,128)S(1)} fusion(bf16[2,16,60,128]{3,0,2,1:T(2,128)(2,1)S(1)} %bitcast.196, f32[1,16,32]{2,1,0:T(8,128)S(1)} %get-tuple-element.46, f32[1,16,32]{2,1,0:T(8,128)S(1)} %get-tuple-element.47), kind=kOutput, calls=%fused_computation.17 | convolution fusion | flops 94372864 | bytes 4427776 | tf_op jit(solution)/shard_map/...ab,caf->...cfb/dot_general | solution.py:47
  58.8 0.8 multiply_add_fusion.1
  59.6 0.4 maximum_bitcast_fusion.1
  60.0 5.0 %fusion.8 = f32[2,60,2,32,128]{4,1,3,2,0:T(8,128)S(1)} fusion(f32[2,60,2,32,128,1]{4,3,1,0,2,5:T(8,128)S(1)} %maximum_bitcast_fusion.1, f32[1,2,128,128]{3,2,0,1:T(8,128)S(1)} %get-tuple-element.22, f32[1,2,128,128]{3,2,0,1:T(8,128)S(1)} %get-tuple-element.32), kind=kOutput, calls=%fused_computation.10 | convolution fusion | flops 1510014976 | bytes 8126464 | tf_op jit(solution)/shard_map/...cfb,cdbk->...dfk/dot_general | solution.py:57
  65.0 1.0 multiply_subtract_fusion.3
  65.9 0.1 maximum_bitcast_fusion.2
  66.1 0.2 maximum_bitcast_fusion.3
  66.4 0.4 maximum_bitcast_fusion
  66.8 0.4 copy-done.6
  67.3 4.5 %fusion.14 = f32[2,60,2,32,128]{4,3,1,0,2:T(8,128)S(1)} fusion(f32[2,60,2,32,128,1]{4,1,3,2,0,5:T(8,128)S(1)} %maximum_bitcast_fusion, f32[1,2,128,128]{3,2,1,0:T(8,128)S(1)} %copy-done.7, f32[1,2,128,128]{3,2,1,0:T(8,128)S(1)} %copy-done.6), kind=kOutput, calls=%fused_computation.16 | convolution fusion | flops 1510014976 | bytes 8126464 | tf_op jit(solution)/shard_map/...cfk,cdkb->...dfb/dot_general | solution.py:62
  71.8 0.6 multiply_subtract_fusion
  72.4 1.3 %fusion.41 = bf16[2,60,16,128]{3,2,1,0:T(8,128)(2,1)S(1)} fusion(f32[2,60,1,32,128]{4,3,1,0,2:T(8,128)S(1)} %get-tuple-element.10, f32[2,60,1,32,128]{4,3,1,0,2:T(8,128)S(1)} %get-tuple-element.9, f32[1,16,32]{2,1,0:T(8,128)S(1)} %get-tuple-element.46, f32[1,16,32]{2,1,0:T(8,128)S(1)} %get-tuple-element.47), kind=kOutput, calls=%fused_computation.44 | convolution fusion | flops 95847424 | bytes 4427776 | tf_op jit(solution)/shard_map/...cfb,caf->...ab/dot_general | solution.py:72
  73.7 0.8 copy.89
  74.6 2.8 %reshape.225 = bf16[16,2,7680]{2,1,0:T(2,128)(2,1)S(1)} reshape(bf16[2048,2,60]{2,1,0:T(2,128)(2,1)S(1)} %bitcast.182) | data formatting | bytes 983040
  77.4 17.7 %all_to_all.30 = bf16[16,2,7680]{2,1,0:T(2,128)(2,1)S(1)} all-to-all(bf16[16,2,7680]{2,1,0:T(2,128)(2,1)S(1)} %reshape.225), channel_id=1, replica_groups=mesh['grp'=2,'ctx'=16] {'ctx'}, dimensions={0} | all-to-all | bytes 983040 | tf_op jit(solution)/shard_map/all_to_all | solution.py:111
  95.0 3.5 %reshape.226 = bf16[2048,2,60]{2,1,0:T(2,128)(2,1)S(1)} reshape(bf16[16,2,7680]{2,1,0:T(2,128)(2,1)S(1)} %all_to_all.30) | data formatting | bytes 983040
  98.6 0.8 copy.88
  99.6 0.6 rev.8
  100.2 0.2 copy.64
  100.4 2.0 %fusion.46 = bf16[960,128]{1,0:T(8,128)(2,1)} fusion(f32[3,960,128]{2,1,0:T(8,128)} %copy-done, f32[960,128]{1,0:T(8,128)S(1)} %reshape.208, f32[3,960,128]{2,1,0:T(8,128)} %copy-done.1, bf16[960,128]{1,0:T(8,128)(2,1)S(1)} %rev.8), kind=kLoop, calls=%fused_computation.59 | loop fusion | flops 614400 | bytes 1966080 | tf_op jit(solution)/shard_map/convert_element_type | solution.py:116
  (54 shorter events, 0.9 us)
Async XLA Ops:
  1.3 5.9 %copy-start.8 = (f32[3,960,7]{1,2,0:T(8,128)S(1)}, f32[3,960,7]{1,2,0:T(8,128)}, u32[]{:S(2)}) copy-start(f32[3,960,7]{1,2,0:T(8,128)} %param.8) | copy-start | bytes 241924
  1.6 16.6 %copy-start.5 = (bf16[60,2048]{1,0:T(8,128)(2,1)S(1)}, bf16[60,2048]{1,0:T(8,128)(2,1)}, u32[]{:S(2)}) copy-start(bf16[60,2048]{1,0:T(8,128)(2,1)} %param.9) | copy-start | bytes 737284
  1.9 16.8 %collective-permute-start.1 = (bf16[3,960,6]{1,2,0:T(8,128)(2,1)S(1)}, bf16[3,960,6]{1,2,0:T(8,128)(2,1)S(1)}, u32[]{:S(2)}, u32[]{:S(2)}) collective-permute-start(bf16[3,960,6]{1,2,0:T(8,128)(2,1)S(1)} %copy.51), channel_id=1, source_target_pairs={{1,0},{2,1},{3,2},{4,3},{5,4},{6,5},{7,6},{8,7},{9,8},{10,9},{11,1... | collective-permute-start | bytes 103688 | tf_op jit(solution)/shard_map/ppermute | solution.py:19
  3.5 14.7 %collective-permute-start = (bf16[3,960,6]{1,2,0:T(8,128)(2,1)S(1)}, bf16[3,960,6]{1,2,0:T(8,128)(2,1)S(1)}, u32[]{:S(2)}, u32[]{:S(2)}) collective-permute-start(bf16[3,960,6]{1,2,0:T(8,128)(2,1)S(1)} %copy.47), channel_id=1, source_target_pairs={{0,1},{1,2},{2,3},{3,4},{4,5},{5,6},{6,7},{7,8},{8,9},{9,10},{10,1... | collective-permute-start | bytes 103688 | tf_op jit(solution)/shard_map/ppermute | solution.py:18
  6.9 13.0 %copy-start.2 = (bf16[960,128]{1,0:T(8,128)(2,1)S(1)}, bf16[960,128]{1,0:T(8,128)(2,1)}, u32[]{:S(2)}) copy-start(bf16[960,128]{1,0:T(8,128)(2,1)} %param.7) | copy-start | bytes 737284
  6.9 13.0 %copy-start.3 = (bf16[960,128]{1,0:T(8,128)(2,1)S(1)}, bf16[960,128]{1,0:T(8,128)(2,1)}, u32[]{:S(2)}) copy-start(bf16[960,128]{1,0:T(8,128)(2,1)} %param.6) | copy-start | bytes 737284
  6.9 13.0 %copy-start.4 = (bf16[960,128]{1,0:T(8,128)(2,1)S(1)}, bf16[960,128]{1,0:T(8,128)(2,1)}, u32[]{:S(2)}) copy-start(bf16[960,128]{1,0:T(8,128)(2,1)} %param.5) | copy-start | bytes 737284
  19.9 2.6 %copy-start.13 = (f32[3,960]{1,0:T(4,128)S(1)}, f32[3,960]{1,0:T(4,128)}, u32[]{:S(2)}) copy-start(f32[3,960]{1,0:T(4,128)} %get-tuple-element.40) | copy-start | bytes 34564
  19.9 2.6 %copy-start.14 = (f32[3,960]{1,0:T(4,128)S(1)}, f32[3,960]{1,0:T(4,128)}, u32[]{:S(2)}) copy-start(f32[3,960]{1,0:T(4,128)} %get-tuple-element.41) | copy-start | bytes 34564
  19.9 2.6 %copy-start.15 = (f32[3,960]{1,0:T(4,128)S(1)}, f32[3,960]{1,0:T(4,128)}, u32[]{:S(2)}) copy-start(f32[3,960]{1,0:T(4,128)} %get-tuple-element.44) | copy-start | bytes 34564
  19.9 2.6 %copy-start.16 = (f32[3,960]{1,0:T(4,128)S(1)}, f32[3,960]{1,0:T(4,128)}, u32[]{:S(2)}) copy-start(f32[3,960]{1,0:T(4,128)} %get-tuple-element.45) | copy-start | bytes 34564
  19.9 2.6 %copy-start.17 = (f32[3,960]{1,0:T(4,128)S(1)}, f32[3,960]{1,0:T(4,128)}, u32[]{:S(2)}) copy-start(f32[3,960]{1,0:T(4,128)} %get-tuple-element.42) | copy-start | bytes 34564
  19.9 2.6 %copy-start.18 = (f32[3,960]{1,0:T(4,128)S(1)}, f32[3,960]{1,0:T(4,128)}, u32[]{:S(2)}) copy-start(f32[3,960]{1,0:T(4,128)} %get-tuple-element.43) | copy-start | bytes 34564
  19.9 2.6 %copy-start.20 = (f32[3,960,1]{1,0,2:T(4,128)S(1)}, f32[3,960,1]{1,0,2:T(4,128)}, u32[]{:S(2)}) copy-start(f32[3,960,1]{1,0,2:T(4,128)} %copy.139) | copy-start | bytes 34564
  22.5 6.4 %copy-start.9 = (f32[3,960]{1,0:T(4,128)S(1)}, f32[3,960]{1,0:T(4,128)}, u32[]{:S(2)}) copy-start(f32[3,960]{1,0:T(4,128)} %get-tuple-element.38) | copy-start | bytes 34564
  22.5 6.4 %copy-start.10 = (f32[3,960]{1,0:T(4,128)S(1)}, f32[3,960]{1,0:T(4,128)}, u32[]{:S(2)}) copy-start(f32[3,960]{1,0:T(4,128)} %get-tuple-element.39) | copy-start | bytes 34564
  22.6 6.4 %copy-start.11 = (f32[3,960]{1,0:T(4,128)S(1)}, f32[3,960]{1,0:T(4,128)}, u32[]{:S(2)}) copy-start(f32[3,960]{1,0:T(4,128)} %get-tuple-element.36) | copy-start | bytes 34564
  22.6 6.4 %copy-start.12 = (f32[3,960]{1,0:T(4,128)S(1)}, f32[3,960]{1,0:T(4,128)}, u32[]{:S(2)}) copy-start(f32[3,960]{1,0:T(4,128)} %get-tuple-element.37) | copy-start | bytes 34564
  22.6 6.4 %copy-start.19 = (f32[3,960,1]{1,0,2:T(4,128)S(1)}, f32[3,960,1]{1,0,2:T(4,128)}, u32[]{:S(2)}) copy-start(f32[3,960,1]{1,0,2:T(4,128)} %copy.140) | copy-start | bytes 34564
  27.1 1.1 %copy-start = (f32[3,960,128]{2,1,0:T(8,128)}, f32[3,960,128]{2,1,0:T(8,128)S(1)}, u32[]{:S(2)}) copy-start(f32[3,960,128]{2,1,0:T(8,128)S(1)} %fusion.31) | copy-start | bytes 4423684
  33.3 1.1 %copy-start.1 = (f32[3,960,128]{2,1,0:T(8,128)}, f32[3,960,128]{2,1,0:T(8,128)S(1)}, u32[]{:S(2)}) copy-start(f32[3,960,128]{2,1,0:T(8,128)S(1)} %fusion.25) | copy-start | bytes 4423684
  35.8 21.7 %all-to-all-start = ((bf16[2,960,128]{2,0,1:T(2,128)(2,1)}), bf16[2,960,128]{2,0,1:T(2,128)(2,1)S(1)}, u32[]{:S(2)}, u32[]{:S(2)}) async-start(bf16[2,960,128]{2,0,1:T(2,128)(2,1)} %copy.53), calls=%async_computation | async-start | bytes 983040 | tf_op jit(solution)/shard_map/all_to_all | solution.py:96
  66.3 0.9 copy-start.6
  66.4 1.0 copy-start.7
where the time goes:
time: 103 us; the launch traced here: 102 us
  local copies, waits for them, and re-layouts  26.3 us (26%)
  other arithmetic  20.2 us (20%)
  blocking collectives  17.7 us (17%)
  matrix products  14.7 us (14%)
  starting transfers between devices  12.5 us (12%)
  waiting for transfers between devices  10.4 us (10%)
    unnamed x67, local copies, waits for them, and re-layouts  19.2 us
    all_to_all x1, blocking collectives, on_device(): lax.all_to_all(convolved, 'ctx', split_axis=2, concat_axis=1, tiled=True)  17.7 us
    all_to_all x1, waiting for transfers between devices, on_device(): lax.all_to_all(outgoing, 'ctx', split_axis=1, concat_axis=2, tiled=True)  10.4 us
    all_to_all x1, starting transfers between devices, on_device(): lax.all_to_all(outgoing, 'ctx', split_axis=1, concat_axis=2, tiled=True)  8.13 us
    dot_general x2, matrix products, forward(): jnp.einsum('...cfb,cdbk->...dfk', twist, inner_fwd, precision=precise)  6.97 us
    add x1, other arithmetic, on_device(): anticausal + mirrored_taps[:, :, offset, None] * padded[:, :, later:later...  4.54 us
    dot_general x1, matrix products, inverse(): jnp.einsum('...cfk,cdkb->...dfb', spectrum, inner_inv, precision=precise)  4.47 us
    add x1, other arithmetic, on_device(): causal + short_taps[:, :, offset, None] * padded[:, :, begin:begin + tokens]  4.31 us
  transfers between devices with their start and end apart: 3, of which 1 were waited for; matrix products, arithmetic and copies ran while one was open for 15% of the time, Pallas kernels for 0%

commit v1 on v0

--- a/solution.py
+++ b/solution.py
@@ -6,6 +6,28 @@
 
 TAPS = 7
 precise = lax.Precision.HIGH
+
+
+def in_blocks(x, dim, size):
+    before, after = (x.shape[:dim], x.shape[dim + 1 :])
+    return jnp.moveaxis(x.reshape(*before, size, -1, *after), dim, 0)
+
+
+def laid_out(blocks, dim):
+    dims = list(blocks.shape[1:])
+    dims[dim] *= blocks.shape[0]
+    return jnp.moveaxis(blocks, 0, dim).reshape(dims)
+
+
+def exchange_in_pairs(x, axis, split_dim, concat_dim):
+    count, mine = (lax.axis_size(axis), lax.axis_index(axis))
+    tiles = in_blocks(x, split_dim, count)
+    done = [tiles[mine]]
+    for step in range(1, count):
+        sent = tiles[mine ^ step]
+        done.append(lax.ppermute(sent, axis, [(i, i ^ step) for i in range(count)]))
+    tiles = jnp.stack(done)[mine ^ jnp.arange(count)]
+    return laid_out(tiles, concat_dim)
 
 
 def with_halo(value, sides, width):
@@ -93,7 +115,7 @@
     product_b = (anticausal[1] * anticausal[2]).astype(jnp.bfloat16)
     tables = fourier_tables(long_filter.shape[1])
     outgoing = jnp.stack([product_a, product_b[::-1]])
-    channel_rows = lax.all_to_all(outgoing, "ctx", split_axis=1, concat_axis=2, tiled=True)
+    channel_rows = exchange_in_pairs(outgoing, "ctx", 1, 2)
     filter_spec = forward(long_filter.astype(jnp.float32), tables)
     data_spec = forward(channel_rows.astype(jnp.float32), tables)
     filter_real = filter_spec[:, 0]

time: 103 us -> 125 us (1.21)
  starting transfers between devices: 12.5 us -> 28.8 us
  local copies, waits for them, and re-layouts: 26.3 us -> 32.8 us
  waiting for transfers between devices: 10.4 us -> 4.95 us
  other arithmetic: 20.2 us -> 23.5 us
    ppermute x0 -> x15, starting transfers between devices: none -> 24.5 us  [exchange_in_pairs(): done.append(lax.ppermute(sent, axis, [(i, i ^ step) for i in range(count)]))]
    all_to_all x1 -> x0, waiting for transfers between devices: 10.4 us -> none  [on_device(): lax.all_to_all(outgoing, 'ctx', split_axis=1, concat_axis=2, tiled=True)]
    all_to_all x1 -> x0, starting transfers between devices: 8.13 us -> none  [on_device(): lax.all_to_all(outgoing, 'ctx', split_axis=1, concat_axis=2, tiled=True)]
    ppermute x0 -> x15, waiting for transfers between devices: none -> 4.94 us  [exchange_in_pairs(): done.append(lax.ppermute(sent, axis, [(i, i ^ step) for i in range(count)]))]
    rev x1, local copies, waits for them, and re-layouts: 0.6 us -> 4.31 us  [on_device(): outgoing = jnp.stack([product_a, product_b[::-1]])]
    add x1, other arithmetic: 4.31 us -> 6.07 us  [on_device(): causal + short_taps[:, :, offset, None] * padded[:, :, begin:begin + tokens]]
    gather x0 -> x1, local copies, waits for them, and re-layouts: none -> 1.66 us  [exchange_in_pairs(): tiles = jnp.stack(done)[mine ^ jnp.arange(count)]]
    dot_general x2, matrix products: 6.97 us -> 8.33 us  [forward(): jnp.einsum('...cfb,cdbk->...dfk', twist, inner_fwd, precision=precise)]
  transfers between devices with their start and end apart: 3 -> 17, of which waited for: 1 -> 2; matrix products, arithmetic and copies ran while one was open for 15% -> 14% of each run, Pallas kernels for 0% -> 0%
where the time goes in v1:
time: 125 us; the launch traced here: 123 us
  local copies, waits for them, and re-layouts  32.8 us (26%)
  starting transfers between devices  28.8 us (23%)
  other arithmetic  23.5 us (19%)
  blocking collectives  16.5 us (13%)
  matrix products  15.8 us (13%)
  waiting for transfers between devices  4.95 us (4%)
    ppermute x15, starting transfers between devices, exchange_in_pairs(): done.append(lax.ppermute(sent, axis, [(i, i ^ step) for i in range(count)]))  24.5 us
    unnamed x85, local copies, waits for them, and re-layouts  19.2 us
    all_to_all x1, blocking collectives, on_device(): lax.all_to_all(convolved, 'ctx', split_axis=2, concat_axis=1, tiled=True)  16.5 us
    dot_general x2, matrix products, forward(): jnp.einsum('...cfb,cdbk->...dfk', twist, inner_fwd, precision=precise)  8.33 us
    add x1, other arithmetic, on_device(): causal + short_taps[:, :, offset, None] * padded[:, :, begin:begin + tokens]  6.07 us
    ppermute x15, waiting for transfers between devices, exchange_in_pairs(): done.append(lax.ppermute(sent, axis, [(i, i ^ step) for i in range(count)]))  4.94 us
    add x1, other arithmetic, on_device(): anticausal + mirrored_taps[:, :, offset, None] * padded[:, :, later:later...  4.54 us
    rev x1, local copies, waits for them, and re-layouts, on_device(): outgoing = jnp.stack([product_a, product_b[::-1]])  4.31 us
  transfers between devices with their start and end apart: 17, of which 2 were waited for; matrix products, arithmetic and copies ran while one was open for 14% of the time, Pallas kernels for 0%

profile of v1, /device:TPU:0, one launch (start us, length us, event | category | flops | bytes accessed | tf_op | source)
XLA Modules:
  0.0 123.4 jit_solution(13612753143195840623)
XLA Ops:
  0.0 1.3 %pad_maximum_fusion.2 = bf16[3,960,128]{2,1,0:T(8,128)(2,1)S(1)} fusion(bf16[1,960,128]{2,1,0:T(8,128)(2,1)} %bitcast.260, bf16[1,960,128]{2,1,0:T(8,128)(2,1)} %bitcast.264, bf16[1,960,128]{2,1,0:T(8,128)(2,1)} %bitcast.268), kind=kLoop, calls=%fused_computation.56 | loop fusion | flops 737280 | bytes 1474560 | tf_op jit(solution)/shard_map/stack | solution.py:102
  1.3 0.3 fusion.95
  1.6 0.3 copy.81
  1.9 1.3 %collective-permute-start.1 = (bf16[3,960,6]{1,2,0:T(8,128)(2,1)S(1)}, bf16[3,960,6]{1,2,0:T(8,128)(2,1)S(1)}, u32[]{:S(2)}, u32[]{:S(2)}) collective-permute-start(bf16[3,960,6]{1,2,0:T(8,128)(2,1)S(1)} %copy.81), channel_id=1, source_target_pairs={{1,0},{2,1},{3,2},{4,3},{5,4},{6,5},{7,6},{8,7},{9,8},{10,9},{11,1... | collective-permute-start | bytes 103688 | tf_op jit(solution)/shard_map/ppermute | solution.py:41
  3.2 0.3 copy.77
  3.5 3.0 %collective-permute-start = (bf16[3,960,6]{1,2,0:T(8,128)(2,1)S(1)}, bf16[3,960,6]{1,2,0:T(8,128)(2,1)S(1)}, u32[]{:S(2)}, u32[]{:S(2)}) collective-permute-start(bf16[3,960,6]{1,2,0:T(8,128)(2,1)S(1)} %copy.77), channel_id=1, source_target_pairs={{0,1},{1,2},{2,3},{3,4},{4,5},{5,6},{6,7},{7,8},{8,9},{9,10},{10,1... | collective-permute-start | bytes 103688 | tf_op jit(solution)/shard_map/ppermute | solution.py:40
  7.3 0.7 reverse.8
  8.2 0.7 reverse.7
  9.0 0.7 reverse.12
  9.9 0.7 reverse.11
  10.7 0.7 reverse.10
  11.5 0.6 copy_bitcast_fusion.24
  12.2 0.7 reverse.9
  13.0 0.6 copy_bitcast_fusion.15
  13.6 0.6 copy_bitcast_fusion.19
  14.3 0.6 copy_bitcast_fusion.17
  14.9 0.7 convolution_bitcast_fusion.1
  15.6 0.3 multiply_add_fusion.4
  16.1 0.7 fusion.60
  16.8 3.4 %fusion.17 = f32[60,2,32,128]{3,0,2,1:T(8,128)} fusion(f32[60,2,32,128]{3,2,0,1:T(8,128)S(1)} %pad_maximum_fusion, f32[1,2,128,128]{3,2,0,1:T(8,128)S(1)} %get-tuple-element.38, f32[1,2,128,128]{3,2,0,1:T(8,128)S(1)} %get-tuple-element.48), kind=kOutput, calls=%fused_computation.26 | convolution fusion | flops 755040256 | bytes 4194304 | tf_op jit(solution)/shard_map/...cfb,cdbk->...dfk/dot_general | solution.py:79
  20.2 0.6 pad_clamp_fusion
  20.8 0.6 copy.216
  21.4 0.7 reverse.13
  22.2 0.6 copy.215
  22.9 0.4 copy.78
  23.3 1.2 copy.82
  24.6 2.6 %maximum_maximum_fusion = (bf16[3,960,134]{2,1,0:T(8,128)(2,1)S(1)}, bf16[3,960,134]{2,1,0:T(8,128)(2,1)S(1)}) fusion(bf16[1,960,128]{2,1,0:T(8,128)(2,1)S(1)} %bitcast.261, bf16[1,960,128]{2,1,0:T(8,128)(2,1)S(1)} %bitcast.265, bf16[1,960,128]{2,1,0:T(8,128)(2,1)S(1)} %bitcast.270, bf16[3,960,6]{2,1,0:T(8,128)(2,1)S(1)} %copy.78, bf16[3,960,6]{2,1,0:T(8,128)(2,1)} %copy.82), kind=kLoop, calls=%fused_computation.40 | loop fusion | flops 6174720 | bytes 2350080 | tf_op jit(solution)/shard_map/concatenate | solution.py:42
  27.3 4.5 %fusion.31 = f32[3,960,128]{2,1,0:T(8,128)S(1)} fusion(bf16[3,960,134]{2,1,0:T(8,128)(2,1)S(1)} %get-tuple-element.16, f32[3,960]{1,0:T(4,128)S(1)} %copy-done.15, f32[3,960]{1,0:T(4,128)S(1)} %copy-done.16, f32[3,960]{1,0:T(4,128)S(1)} %copy-done.19, f32[3,960]{1,0:T(4,128)S(1)} %copy-done.20, f32[3,960]{1,0:T(4,128)S(1)} %copy-done.17, ...), kind=kLoop, calls=%fused_computation.39 | loop fusion | flops 8110080 | bytes 6716160 | tf_op jit(solution)/shard_map/add | solution.py:112
  31.8 0.7 fusion.55
  32.6 4.3 %rev.7 = bf16[960,128]{1,0:T(8,128)(2,1)} reverse(bf16[960,128]{1,0:T(8,128)(2,1)} %fusion.55), dimensions={0} | reverse | bytes 491520 | tf_op jit(solution)/shard_map/rev | solution.py:117
  36.9 1.7 %stack.163 = bf16[1,16,60,128]{3,2,1,0:T(8,128)(2,1)} reshape(bf16[960,128]{1,0:T(8,128)(2,1)} %rev.7) | data formatting | bytes 491520 | tf_op jit(solution)/shard_map/stack | solution.py:117
  38.6 6.1 %fusion.25 = f32[3,960,128]{2,1,0:T(8,128)S(1)} fusion(bf16[3,960,134]{2,1,0:T(8,128)(2,1)S(1)} %get-tuple-element.15, f32[3,960]{1,0:T(4,128)S(1)} %get-tuple-element.50, f32[3,960]{1,0:T(4,128)S(1)} %get-tuple-element.51, f32[3,960]{1,0:T(4,128)} %get-tuple-element.52, f32[3,960]{1,0:T(4,128)} %get-tuple-element.53, f32[3,960]{1,0:T(4,128)S(1)} %get-tuple-element.54, ...), kind=kLoop, calls=%fused_computation.33 | loop fusion | flops 8110080 | bytes 6716160 | tf_op jit(solution)/shard_map/add | solution.py:109
  44.7 1.1 copy-done.1
  45.9 0.8 copy-done.10
  47.2 2.7 %collective-permute-start.2 = (bf16[2,60,128]{2,0,1:T(2,128)(2,1)S(1)}, bf16[2,60,128]{2,0,1:T(2,128)(2,1)S(1)}, u32[]{:S(2)}, u32[]{:S(2)}) collective-permute-start(bf16[2,60,128]{2,0,1:T(2,128)(2,1)S(1)} %bitcast.299), channel_id=1, source_target_pairs={{0,1},{1,0},{2,3},{3,2},{4,5},{5,4},{6,7},{7,6},{8,9},{9,8},{10,11... | collective-permute-start | bytes 92168 | tf_op jit(solution)/shard_map/ppermute | solution.py:28
  49.8 2.4 %collective-permute-start.3 = (bf16[2,60,128]{2,0,1:T(2,128)(2,1)S(1)}, bf16[2,60,128]{2,0,1:T(2,128)(2,1)S(1)}, u32[]{:S(2)}, u32[]{:S(2)}) collective-permute-start(bf16[2,60,128]{2,0,1:T(2,128)(2,1)S(1)} %bitcast.297), channel_id=1, source_target_pairs={{0,2},{1,3},{2,0},{3,1},{4,6},{5,7},{6,4},{7,5},{8,10},{9,11},{10,... | collective-permute-start | bytes 92168 | tf_op jit(solution)/shard_map/ppermute | solution.py:28
  52.2 1.6 %collective-permute-start.5 = (bf16[2,60,128]{2,0,1:T(2,128)(2,1)S(1)}, bf16[2,60,128]{2,0,1:T(2,128)(2,1)S(1)}, u32[]{:S(2)}, u32[]{:S(2)}) collective-permute-start(bf16[2,60,128]{2,0,1:T(2,128)(2,1)S(1)} %bitcast.293), channel_id=1, source_target_pairs={{0,4},{1,5},{2,6},{3,7},{4,0},{5,1},{6,2},{7,3},{8,12},{9,13},{10,... | collective-permute-start | bytes 92168 | tf_op jit(solution)/shard_map/ppermute | solution.py:28
  54.2 3.0 %collective-permute-start.7 = (bf16[2,60,128]{2,0,1:T(2,128)(2,1)S(1)}, bf16[2,60,128]{2,0,1:T(2,128)(2,1)S(1)}, u32[]{:S(2)}, u32[]{:S(2)}) collective-permute-start(bf16[2,60,128]{2,0,1:T(2,128)(2,1)S(1)} %bitcast.298), channel_id=1, source_target_pairs={{0,6},{1,7},{2,4},{3,5},{4,2},{5,3},{6,0},{7,1},{8,14},{9,15},{10,... | collective-permute-start | bytes 92168 | tf_op jit(solution)/shard_map/ppermute | solution.py:28
  57.4 2.5 %collective-permute-start.9 = (bf16[2,60,128]{2,0,1:T(2,128)(2,1)S(1)}, bf16[2,60,128]{2,0,1:T(2,128)(2,1)S(1)}, u32[]{:S(2)}, u32[]{:S(2)}) collective-permute-start(bf16[2,60,128]{2,0,1:T(2,128)(2,1)S(1)} %bitcast.294), channel_id=1, source_target_pairs={{0,8},{1,9},{2,10},{3,11},{4,12},{5,13},{6,14},{7,15},{8,0},{9,1},... | collective-permute-start | bytes 92168 | tf_op jit(solution)/shard_map/ppermute | solution.py:28
  60.1 3.9 %collective-permute-start.11 = (bf16[2,60,128]{2,0,1:T(2,128)(2,1)S(1)}, bf16[2,60,128]{2,0,1:T(2,128)(2,1)S(1)}, u32[]{:S(2)}, u32[]{:S(2)}) collective-permute-start(bf16[2,60,128]{2,0,1:T(2,128)(2,1)S(1)} %bitcast.290), channel_id=1, source_target_pairs={{0,10},{1,11},{2,8},{3,9},{4,14},{5,15},{6,12},{7,13},{8,2},{9,3},... | collective-permute-start | bytes 92168 | tf_op jit(solution)/shard_map/ppermute | solution.py:28
  64.1 2.5 %collective-permute-start.13 = (bf16[2,60,128]{2,0,1:T(2,128)(2,1)S(1)}, bf16[2,60,128]{2,0,1:T(2,128)(2,1)S(1)}, u32[]{:S(2)}, u32[]{:S(2)}) collective-permute-start(bf16[2,60,128]{2,0,1:T(2,128)(2,1)S(1)} %bitcast.288), channel_id=1, source_target_pairs={{0,12},{1,13},{2,14},{3,15},{4,8},{5,9},{6,10},{7,11},{8,4},{9,5},... | collective-permute-start | bytes 92168 | tf_op jit(solution)/shard_map/ppermute | solution.py:28
  66.7 0.9 collective-permute-start.14
  67.6 3.6 %collective-permute-start.15 = (bf16[2,60,128]{2,0,1:T(2,128)(2,1)S(1)}, bf16[2,60,128]{2,0,1:T(2,128)(2,1)S(1)}, u32[]{:S(2)}, u32[]{:S(2)}) collective-permute-start(bf16[2,60,128]{2,0,1:T(2,128)(2,1)S(1)} %bitcast.286), channel_id=1, source_target_pairs={{0,14},{1,15},{2,12},{3,13},{4,10},{5,11},{6,8},{7,9},{8,6},{9,7},... | collective-permute-start | bytes 92168 | tf_op jit(solution)/shard_map/ppermute | solution.py:28
  71.3 1.3 %collective-permute-start.16 = (bf16[2,60,128]{2,0,1:T(2,128)(2,1)S(1)}, bf16[2,60,128]{2,0,1:T(2,128)(2,1)S(1)}, u32[]{:S(2)}, u32[]{:S(2)}) collective-permute-start(bf16[2,60,128]{2,0,1:T(2,128)(2,1)S(1)} %bitcast.285), channel_id=1, source_target_pairs={{0,15},{1,14},{2,13},{3,12},{4,11},{5,10},{6,9},{7,8},{8,7},{9,6},... | collective-permute-start | bytes 92168 | tf_op jit(solution)/shard_map/ppermute | solution.py:28
  72.7 1.7 %collective-permute-done.15 = bf16[2,60,128]{2,0,1:T(2,128)(2,1)S(1)} collective-permute-done((bf16[2,60,128]{2,0,1:T(2,128)(2,1)S(1)}, bf16[2,60,128]{2,0,1:T(2,128)(2,1)S(1)}, u32[]{:S(2)}, u32[]{:S(2)}) %collective-permute-start.15) | collective-permute-done | bytes 30752 | tf_op jit(solution)/shard_map/ppermute | solution.py:28
  74.4 3.2 %collective-permute-done.16 = bf16[2,60,128]{2,0,1:T(2,128)(2,1)S(1)} collective-permute-done((bf16[2,60,128]{2,0,1:T(2,128)(2,1)S(1)}, bf16[2,60,128]{2,0,1:T(2,128)(2,1)S(1)}, u32[]{:S(2)}, u32[]{:S(2)}) %collective-permute-start.16) | collective-permute-done | bytes 30752 | tf_op jit(solution)/shard_map/ppermute | solution.py:28
  77.7 1.7 %gather_fusion = bf16[16,2,60,128]{3,1,2,0:T(2,128)(2,1)S(1)} fusion(bf16[16,2,60,128]{3,1,2,0:T(2,128)(2,1)S(1)} %constant_dynamic-update-slice_fusion.2, s32[1024]{0:T(1024)} %pad_clamp_fusion), kind=kCustom, calls=%fused_computation | custom fusion | bytes 983104 | tf_op jit(solution)/shard_map/gather | solution.py:29
  79.4 1.2 convolution_bitcast_fusion
  80.6 0.8 multiply_add_fusion.1
  81.4 0.4 maximum_bitcast_fusion.1
  81.8 0.5 copy-done.7
  82.4 5.0 %fusion.8 = f32[2,60,2,32,128]{4,1,3,2,0:T(8,128)S(1)} fusion(f32[2,60,2,32,128,1]{4,3,1,0,2,5:T(8,128)S(1)} %maximum_bitcast_fusion.1, f32[1,2,128,128]{3,2,0,1:T(8,128)S(1)} %copy-done.7, f32[1,2,128,128]{3,2,0,1:T(8,128)S(1)} %copy-done.9), kind=kOutput, calls=%fused_computation.11 | convolution fusion | flops 1510014976 | bytes 8126464 | tf_op jit(solution)/shard_map/...cfb,cdbk->...dfk/dot_general | solution.py:79
  87.3 1.2 multiply_subtract_fusion.3
  89.2 0.4 maximum_bitcast_fusion
  89.9 4.3 %fusion.14 = f32[2,60,2,32,128]{4,3,1,0,2:T(8,128)S(1)} fusion(f32[2,60,2,32,128,1]{4,1,3,2,0,5:T(8,128)S(1)} %maximum_bitcast_fusion, f32[1,2,128,128]{3,2,1,0:T(8,128)S(1)} %copy-done.13, f32[1,2,128,128]{3,2,1,0:T(8,128)S(1)} %copy-done.12), kind=kOutput, calls=%fused_computation.17 | convolution fusion | flops 1510014976 | bytes 8126464 | tf_op jit(solution)/shard_map/...cfk,cdkb->...dfb/dot_general | solution.py:84
  94.2 0.6 multiply_subtract_fusion
  94.8 1.3 %fusion.41 = bf16[2,60,16,128]{3,2,1,0:T(8,128)(2,1)S(1)} fusion(f32[2,60,1,32,128]{4,3,1,0,2:T(8,128)S(1)} %get-tuple-element.10, f32[2,60,1,32,128]{4,3,1,0,2:T(8,128)S(1)} %get-tuple-element.9, f32[1,16,32]{2,1,0:T(8,128)S(1)} %get-tuple-element.62, f32[1,16,32]{2,1,0:T(8,128)S(1)} %get-tuple-element.63), kind=kOutput, calls=%fused_computation.45 | convolution fusion | flops 95847424 | bytes 4427776 | tf_op jit(solution)/shard_map/...cfb,caf->...ab/dot_general | solution.py:94
  96.1 0.8 copy.134
  96.9 2.8 %reshape.285 = bf16[16,2,7680]{2,1,0:T(2,128)(2,1)S(1)} reshape(bf16[2048,2,60]{2,1,0:T(2,128)(2,1)S(1)} %bitcast.258) | data formatting | bytes 983040
  99.7 16.5 %all_to_all.15 = bf16[16,2,7680]{2,1,0:T(2,128)(2,1)S(1)} all-to-all(bf16[16,2,7680]{2,1,0:T(2,128)(2,1)S(1)} %reshape.285), channel_id=1, replica_groups=mesh['grp'=2,'ctx'=16] {'ctx'}, dimensions={0} | all-to-all | bytes 983040 | tf_op jit(solution)/shard_map/all_to_all | solution.py:133
  116.2 3.5 %reshape.286 = bf16[2048,2,60]{2,1,0:T(2,128)(2,1)S(1)} reshape(bf16[16,2,7680]{2,1,0:T(2,128)(2,1)S(1)} %all_to_all.15) | data formatting | bytes 983040
  119.7 0.8 copy.133
  120.8 0.6 rev.8
  121.6 1.8 %fusion.46 = bf16[960,128]{1,0:T(8,128)(2,1)} fusion(f32[3,960,128]{2,1,0:T(8,128)S(1)} %fusion.31, f32[960,128]{1,0:T(8,128)S(1)} %reshape.260, f32[3,960,128]{2,1,0:T(8,128)} %copy-done.1, bf16[960,128]{1,0:T(8,128)(2,1)S(1)} %rev.8), kind=kLoop, calls=%fused_computation.60 | loop fusion | flops 614400 | bytes 1966080 | tf_op jit(solution)/shard_map/convert_element_type | solution.py:138
  (121 shorter events, 4.4 us)
Async XLA Ops:
  1.3 6.0 %copy-start.14 = (f32[3,960,7]{1,2,0:T(8,128)S(1)}, f32[3,960,7]{1,2,0:T(8,128)}, u32[]{:S(2)}) copy-start(f32[3,960,7]{1,2,0:T(8,128)} %param.8) | copy-start | bytes 241924
  1.6 11.4 %copy-start.11 = (bf16[60,2048]{1,0:T(8,128)(2,1)S(1)}, bf16[60,2048]{1,0:T(8,128)(2,1)}, u32[]{:S(2)}) copy-start(bf16[60,2048]{1,0:T(8,128)(2,1)} %param.9) | copy-start | bytes 737284
  1.9 21.4 %collective-permute-start.1 = (bf16[3,960,6]{1,2,0:T(8,128)(2,1)S(1)}, bf16[3,960,6]{1,2,0:T(8,128)(2,1)S(1)}, u32[]{:S(2)}, u32[]{:S(2)}) collective-permute-start(bf16[3,960,6]{1,2,0:T(8,128)(2,1)S(1)} %copy.81), channel_id=1, source_target_pairs={{1,0},{2,1},{3,2},{4,3},{5,4},{6,5},{7,6},{8,7},{9,8},{10,9},{11,1... | collective-permute-start | bytes 103688 | tf_op jit(solution)/shard_map/ppermute | solution.py:41
  3.5 19.4 %collective-permute-start = (bf16[3,960,6]{1,2,0:T(8,128)(2,1)S(1)}, bf16[3,960,6]{1,2,0:T(8,128)(2,1)S(1)}, u32[]{:S(2)}, u32[]{:S(2)}) collective-permute-start(bf16[3,960,6]{1,2,0:T(8,128)(2,1)S(1)} %copy.77), channel_id=1, source_target_pairs={{0,1},{1,2},{2,3},{3,4},{4,5},{5,6},{6,7},{7,8},{8,9},{9,10},{10,1... | collective-permute-start | bytes 103688 | tf_op jit(solution)/shard_map/ppermute | solution.py:40
  16.8 3.4 %copy-start.6 = (f32[1,2,128,128]{3,2,0,1:T(8,128)}, f32[1,2,128,128]{3,2,0,1:T(8,128)S(1)}, u32[]{:S(2)}) copy-start(f32[1,2,128,128]{3,2,0,1:T(8,128)S(1)} %get-tuple-element.38) | copy-start | bytes 393220
  16.8 3.4 %copy-start.8 = (f32[1,2,128,128]{3,2,0,1:T(8,128)}, f32[1,2,128,128]{3,2,0,1:T(8,128)S(1)}, u32[]{:S(2)}) copy-start(f32[1,2,128,128]{3,2,0,1:T(8,128)S(1)} %get-tuple-element.48) | copy-start | bytes 393220
  20.2 4.3 %copy-start.2 = (bf16[960,128]{1,0:T(8,128)(2,1)S(1)}, bf16[960,128]{1,0:T(8,128)(2,1)}, u32[]{:S(2)}) copy-start(bf16[960,128]{1,0:T(8,128)(2,1)} %param.7) | copy-start | bytes 737284
  20.2 4.3 %copy-start.3 = (bf16[960,128]{1,0:T(8,128)(2,1)S(1)}, bf16[960,128]{1,0:T(8,128)(2,1)}, u32[]{:S(2)}) copy-start(bf16[960,128]{1,0:T(8,128)(2,1)} %param.6) | copy-start | bytes 737284
  20.2 4.3 %copy-start.4 = (bf16[960,128]{1,0:T(8,128)(2,1)S(1)}, bf16[960,128]{1,0:T(8,128)(2,1)}, u32[]{:S(2)}) copy-start(bf16[960,128]{1,0:T(8,128)(2,1)} %param.5) | copy-start | bytes 737284
  24.5 2.7 %copy-start.5 = (bf16[960,128]{1,0:T(8,128)(2,1)S(1)}, bf16[960,128]{1,0:T(8,128)(2,1)}, u32[]{:S(2)}) copy-start(bf16[960,128]{1,0:T(8,128)(2,1)} %param.5) | copy-start | bytes 737284
  24.5 2.7 %copy-start.15 = (f32[3,960]{1,0:T(4,128)S(1)}, f32[3,960]{1,0:T(4,128)}, u32[]{:S(2)}) copy-start(f32[3,960]{1,0:T(4,128)} %get-tuple-element.56) | copy-start | bytes 34564
  24.5 2.7 %copy-start.16 = (f32[3,960]{1,0:T(4,128)S(1)}, f32[3,960]{1,0:T(4,128)}, u32[]{:S(2)}) copy-start(f32[3,960]{1,0:T(4,128)} %get-tuple-element.57) | copy-start | bytes 34564
  24.5 2.7 %copy-start.17 = (f32[3,960]{1,0:T(4,128)S(1)}, f32[3,960]{1,0:T(4,128)}, u32[]{:S(2)}) copy-start(f32[3,960]{1,0:T(4,128)} %get-tuple-element.60) | copy-start | bytes 34564
  24.5 2.7 %copy-start.18 = (f32[3,960]{1,0:T(4,128)S(1)}, f32[3,960]{1,0:T(4,128)}, u32[]{:S(2)}) copy-start(f32[3,960]{1,0:T(4,128)} %get-tuple-element.61) | copy-start | bytes 34564
  24.6 2.7 %copy-start.19 = (f32[3,960]{1,0:T(4,128)S(1)}, f32[3,960]{1,0:T(4,128)}, u32[]{:S(2)}) copy-start(f32[3,960]{1,0:T(4,128)} %get-tuple-element.58) | copy-start | bytes 34564
  24.6 2.7 %copy-start.20 = (f32[3,960]{1,0:T(4,128)S(1)}, f32[3,960]{1,0:T(4,128)}, u32[]{:S(2)}) copy-start(f32[3,960]{1,0:T(4,128)} %get-tuple-element.59) | copy-start | bytes 34564
  24.6 2.7 %copy-start.21 = (f32[3,960,1]{1,0,2:T(4,128)S(1)}, f32[3,960,1]{1,0,2:T(4,128)}, u32[]{:S(2)}) copy-start(f32[3,960,1]{1,0,2:T(4,128)} %copy.215) | copy-start | bytes 34564
  44.7 1.1 copy-start.1
  45.8 0.9 copy-start.10
  47.2 7.0 %collective-permute-start.2 = (bf16[2,60,128]{2,0,1:T(2,128)(2,1)S(1)}, bf16[2,60,128]{2,0,1:T(2,128)(2,1)S(1)}, u32[]{:S(2)}, u32[]{:S(2)}) collective-permute-start(bf16[2,60,128]{2,0,1:T(2,128)(2,1)S(1)} %bitcast.299), channel_id=1, source_target_pairs={{0,1},{1,0},{2,3},{3,2},{4,5},{5,4},{6,7},{7,6},{8,9},{9,8},{10,11... | collective-permute-start | bytes 92168 | tf_op jit(solution)/shard_map/ppermute | solution.py:28
  49.8 7.4 %collective-permute-start.3 = (bf16[2,60,128]{2,0,1:T(2,128)(2,1)S(1)}, bf16[2,60,128]{2,0,1:T(2,128)(2,1)S(1)}, u32[]{:S(2)}, u32[]{:S(2)}) collective-permute-start(bf16[2,60,128]{2,0,1:T(2,128)(2,1)S(1)} %bitcast.297), channel_id=1, source_target_pairs={{0,2},{1,3},{2,0},{3,1},{4,6},{5,7},{6,4},{7,5},{8,10},{9,11},{10,... | collective-permute-start | bytes 92168 | tf_op jit(solution)/shard_map/ppermute | solution.py:28
  52.2 5.2 %collective-permute-start.4 = (bf16[2,60,128]{2,0,1:T(2,128)(2,1)S(1)}, bf16[2,60,128]{2,0,1:T(2,128)(2,1)S(1)}, u32[]{:S(2)}, u32[]{:S(2)}) collective-permute-start(bf16[2,60,128]{2,0,1:T(2,128)(2,1)S(1)} %bitcast.295), channel_id=1, source_target_pairs={{0,3},{1,2},{2,1},{3,0},{4,7},{5,6},{6,5},{7,4},{8,11},{9,10},{10,... | collective-permute-start | bytes 92168 | tf_op jit(solution)/shard_map/ppermute | solution.py:28
  52.2 7.8 %collective-permute-start.5 = (bf16[2,60,128]{2,0,1:T(2,128)(2,1)S(1)}, bf16[2,60,128]{2,0,1:T(2,128)(2,1)S(1)}, u32[]{:S(2)}, u32[]{:S(2)}) collective-permute-start(bf16[2,60,128]{2,0,1:T(2,128)(2,1)S(1)} %bitcast.293), channel_id=1, source_target_pairs={{0,4},{1,5},{2,6},{3,7},{4,0},{5,1},{6,2},{7,3},{8,12},{9,13},{10,... | collective-permute-start | bytes 92168 | tf_op jit(solution)/shard_map/ppermute | solution.py:28
  53.8 6.3 %collective-permute-start.6 = (bf16[2,60,128]{2,0,1:T(2,128)(2,1)S(1)}, bf16[2,60,128]{2,0,1:T(2,128)(2,1)S(1)}, u32[]{:S(2)}, u32[]{:S(2)}) collective-permute-start(bf16[2,60,128]{2,0,1:T(2,128)(2,1)S(1)} %bitcast.291), channel_id=1, source_target_pairs={{0,5},{1,4},{2,7},{3,6},{4,1},{5,0},{6,3},{7,2},{8,13},{9,12},{10,... | collective-permute-start | bytes 92168 | tf_op jit(solution)/shard_map/ppermute | solution.py:28
  54.2 9.8 %collective-permute-start.7 = (bf16[2,60,128]{2,0,1:T(2,128)(2,1)S(1)}, bf16[2,60,128]{2,0,1:T(2,128)(2,1)S(1)}, u32[]{:S(2)}, u32[]{:S(2)}) collective-permute-start(bf16[2,60,128]{2,0,1:T(2,128)(2,1)S(1)} %bitcast.298), channel_id=1, source_target_pairs={{0,6},{1,7},{2,4},{3,5},{4,2},{5,3},{6,0},{7,1},{8,14},{9,15},{10,... | collective-permute-start | bytes 92168 | tf_op jit(solution)/shard_map/ppermute | solution.py:28
  57.3 6.8 %collective-permute-start.8 = (bf16[2,60,128]{2,0,1:T(2,128)(2,1)S(1)}, bf16[2,60,128]{2,0,1:T(2,128)(2,1)S(1)}, u32[]{:S(2)}, u32[]{:S(2)}) collective-permute-start(bf16[2,60,128]{2,0,1:T(2,128)(2,1)S(1)} %bitcast.296), channel_id=1, source_target_pairs={{0,7},{1,6},{2,5},{3,4},{4,3},{5,2},{6,1},{7,0},{8,15},{9,14},{10,... | collective-permute-start | bytes 92168 | tf_op jit(solution)/shard_map/ppermute | solution.py:28
  57.4 9.2 %collective-permute-start.9 = (bf16[2,60,128]{2,0,1:T(2,128)(2,1)S(1)}, bf16[2,60,128]{2,0,1:T(2,128)(2,1)S(1)}, u32[]{:S(2)}, u32[]{:S(2)}) collective-permute-start(bf16[2,60,128]{2,0,1:T(2,128)(2,1)S(1)} %bitcast.294), channel_id=1, source_target_pairs={{0,8},{1,9},{2,10},{3,11},{4,12},{5,13},{6,14},{7,15},{8,0},{9,1},... | collective-permute-start | bytes 92168 | tf_op jit(solution)/shard_map/ppermute | solution.py:28
  59.9 7.7 %collective-permute-start.10 = (bf16[2,60,128]{2,0,1:T(2,128)(2,1)S(1)}, bf16[2,60,128]{2,0,1:T(2,128)(2,1)S(1)}, u32[]{:S(2)}, u32[]{:S(2)}) collective-permute-start(bf16[2,60,128]{2,0,1:T(2,128)(2,1)S(1)} %bitcast.292), channel_id=1, source_target_pairs={{0,9},{1,8},{2,11},{3,10},{4,13},{5,12},{6,15},{7,14},{8,1},{9,0},... | collective-permute-start | bytes 92168 | tf_op jit(solution)/shard_map/ppermute | solution.py:28
  60.1 11.2 %collective-permute-start.11 = (bf16[2,60,128]{2,0,1:T(2,128)(2,1)S(1)}, bf16[2,60,128]{2,0,1:T(2,128)(2,1)S(1)}, u32[]{:S(2)}, u32[]{:S(2)}) collective-permute-start(bf16[2,60,128]{2,0,1:T(2,128)(2,1)S(1)} %bitcast.290), channel_id=1, source_target_pairs={{0,10},{1,11},{2,8},{3,9},{4,14},{5,15},{6,12},{7,13},{8,2},{9,3},... | collective-permute-start | bytes 92168 | tf_op jit(solution)/shard_map/ppermute | solution.py:28
  64.0 8.6 %collective-permute-start.12 = (bf16[2,60,128]{2,0,1:T(2,128)(2,1)S(1)}, bf16[2,60,128]{2,0,1:T(2,128)(2,1)S(1)}, u32[]{:S(2)}, u32[]{:S(2)}) collective-permute-start(bf16[2,60,128]{2,0,1:T(2,128)(2,1)S(1)} %bitcast.289), channel_id=1, source_target_pairs={{0,11},{1,10},{2,9},{3,8},{4,15},{5,14},{6,13},{7,12},{8,3},{9,2},... | collective-permute-start | bytes 92168 | tf_op jit(solution)/shard_map/ppermute | solution.py:28
  64.1 8.5 %collective-permute-start.13 = (bf16[2,60,128]{2,0,1:T(2,128)(2,1)S(1)}, bf16[2,60,128]{2,0,1:T(2,128)(2,1)S(1)}, u32[]{:S(2)}, u32[]{:S(2)}) collective-permute-start(bf16[2,60,128]{2,0,1:T(2,128)(2,1)S(1)} %bitcast.288), channel_id=1, source_target_pairs={{0,12},{1,13},{2,14},{3,15},{4,8},{5,9},{6,10},{7,11},{8,4},{9,5},... | collective-permute-start | bytes 92168 | tf_op jit(solution)/shard_map/ppermute | solution.py:28
  66.7 6.0 %collective-permute-start.14 = (bf16[2,60,128]{2,0,1:T(2,128)(2,1)S(1)}, bf16[2,60,128]{2,0,1:T(2,128)(2,1)S(1)}, u32[]{:S(2)}, u32[]{:S(2)}) collective-permute-start(bf16[2,60,128]{2,0,1:T(2,128)(2,1)S(1)} %bitcast.287), channel_id=1, source_target_pairs={{0,13},{1,12},{2,15},{3,14},{4,9},{5,8},{6,11},{7,10},{8,5},{9,4},... | collective-permute-start | bytes 92168 | tf_op jit(solution)/shard_map/ppermute | solution.py:28
  67.6 6.8 %collective-permute-start.15 = (bf16[2,60,128]{2,0,1:T(2,128)(2,1)S(1)}, bf16[2,60,128]{2,0,1:T(2,128)(2,1)S(1)}, u32[]{:S(2)}, u32[]{:S(2)}) collective-permute-start(bf16[2,60,128]{2,0,1:T(2,128)(2,1)S(1)} %bitcast.286), channel_id=1, source_target_pairs={{0,14},{1,15},{2,12},{3,13},{4,10},{5,11},{6,8},{7,9},{8,6},{9,7},... | collective-permute-start | bytes 92168 | tf_op jit(solution)/shard_map/ppermute | solution.py:28
  71.3 6.4 %collective-permute-start.16 = (bf16[2,60,128]{2,0,1:T(2,128)(2,1)S(1)}, bf16[2,60,128]{2,0,1:T(2,128)(2,1)S(1)}, u32[]{:S(2)}, u32[]{:S(2)}) collective-permute-start(bf16[2,60,128]{2,0,1:T(2,128)(2,1)S(1)} %bitcast.285), channel_id=1, source_target_pairs={{0,15},{1,14},{2,13},{3,12},{4,11},{5,10},{6,9},{7,8},{8,7},{9,6},... | collective-permute-start | bytes 92168 | tf_op jit(solution)/shard_map/ppermute | solution.py:28
  81.4 0.9 copy-start.7
  81.4 1.0 copy-start.9
  82.4 5.0 %copy-start = (f32[60,2,32,128]{3,0,2,1:T(8,128)S(1)}, f32[60,2,32,128]{3,0,2,1:T(8,128)}, u32[]{:S(2)}) copy-start(f32[60,2,32,128]{3,0,2,1:T(8,128)} %fusion.17) | copy-start | bytes 5898244
  88.9 0.9 copy-start.12
  88.9 1.0 copy-start.13
